TPU v7x, 128 devices: a whole 4x4x4 slice. The times are simulated.
128 devices in a mesh: lr: 16 (over x, y), lc: 8 (over z, core).
Axes of the slice: x: 4, y: 4, z: 4, core: 2. Of those that a mesh axis runs over, the one named last changes fastest.
Arguments:
- queries: bfloat16 [8192, 768], P(('lr', 'lc')), may hold values from -6 to 6
- probes: int32 [8192, 16], P(('lr', 'lc')), may hold values from 0 to 1023, as said below
- assign: int32 [8192], P(('lr', 'lc')), may hold values from 0 to 1023, as said below
- list_rows: bfloat16 [1024, 1024, 768], P(('lr', 'lc')), may hold values from -0.21875 to 0.21875
- list_fill: int32 [1024], P(('lr', 'lc')), may hold values from 1 to 1024
- centroids: float32 [1024, 768], P(('lr', 'lc')), may hold values from -6 to 6
- list_sums: float32 [1024, 768], P(('lr', 'lc')), may hold values from -6 to 6
Outputs:
- dup_max: float32 [8192, 16], P(('lr', 'lc'))
- codes: bfloat16 [1024, 32, 768], P(('lr', 'lc'))
- scales: float32 [1024, 32], P(('lr', 'lc'))
- new_sums: float32 [1024, 768], P(('lr', 'lc'))
Inputs may be any that keep to these rules, and one draw needn't show every extreme that they name: A list id is 8 times its owner's device index along lr+lc plus its place there. The probe pairs of one device's new vectors name lists of one owner at most 16 times, and one list is named by at most 256 pairs over all new vectors; both bounds are reached. A vector's probes may repeat a list. `assign`: one device's new vectors go to lists of one owner at most 2 times, and one list receives at most 32 new vectors; both bounds are reached.
All inputs are finite; a program needn't handle non-finite values. Where the computation divides by a largest or mean magnitude, that divisor is 1e-20 or more.
Results may differ from a plain program's by a relative error of at most 0.001.
Values may be sent and summed in bfloat16 or wider, within the bound.
A program may use at most 64 MiB of HBM per device.

v0:
```python
import functools

import jax
import jax.numpy as jnp
from jax import lax
from jax.experimental import pallas as pl
from jax.experimental.pallas import tpu as pltpu
from jax.sharding import PartitionSpec as P

BF16, F32, I32 = jnp.bfloat16, jnp.float32, jnp.int32
ROW = (((1,), (1,)), ((), ()))
COL = (((0,), (0,)), ((), ()))


def iota(shape, axis):
    return lax.broadcasted_iota(I32, shape, axis)


def mask(cond):
    return jnp.where(cond, 1.0, 0.0).astype(BF16)


def mm(a, b, dims=(((1,), (0,)), ((), ()))):
    return lax.dot_general(a, b, dims, preferred_element_type=F32)


def split(x):
    hi = x.astype(BF16)
    rest = x - hi.astype(F32)
    mid = rest.astype(BF16)
    return hi, mid, (rest - mid.astype(F32)).astype(BF16)


def columns(table):
    return jnp.concatenate([table[:, j : j + 1] for j in range(table.shape[1])], axis=0)


def uncolumns(column, count):
    rows = column.shape[0] // count
    lane = iota((rows, count), 1)
    out = jnp.zeros((rows, count), column.dtype)
    for j in range(count):
        out = jnp.where(lane == j, column[j * rows : (j + 1) * rows], out)
    return out


def rank_by_owner(owners, group_size):
    count = owners.shape[0]
    hot = mask(owners == iota((count, group_size), 1))
    earlier = mask(iota((count, count), 1) < iota((count, count), 0))
    before = mm(earlier, hot)
    rank = jnp.sum(before * hot.astype(F32), axis=1, keepdims=True).astype(I32)
    return hot, rank


def route_kernel(probes_ref, assign_ref, table_ref, rank_ref, *, group_size, list_count, caps):
    cap, cap2 = caps
    query_count, probe_count = probes_ref.shape
    lists = columns(probes_ref[...])
    pair_count = query_count * probe_count
    hot, rank = rank_by_owner(lists // list_count, group_size)
    rank_ref[...] = uncolumns(rank, probe_count)
    lane = iota((pair_count, 128), 1)
    query = (iota((pair_count, 1), 0) % query_count).astype(F32)
    place = (lists % list_count + 1).astype(F32)
    values = jnp.where(lane == rank, query, 0.0) + jnp.where(lane == rank + cap, place, 0.0)
    table = mm(hot, values.astype(BF16), COL)

    ids = assign_ref[...]
    hot2, rank2 = rank_by_owner(ids // list_count, group_size)
    lane2 = iota((query_count, 128), 1) - 2 * cap
    query2 = iota((query_count, 1), 0).astype(F32)
    place2 = (ids % list_count + 1).astype(F32)
    values2 = jnp.where(lane2 == rank2, query2, 0.0) + jnp.where(lane2 == rank2 + cap2, place2, 0.0)
    table_ref[...] = table + mm(hot2, values2.astype(BF16), COL)


def score_kernel(fill_ref, lists_ref, vec_ref, rows_ref, best_ref, bucket_ref, *, per_list):
    which = pl.program_id(0)
    slots = lists_ref.shape[1]
    lanes = 128

    @pl.when(which == 0)
    def _():
        count = pl.num_programs(0)
        best_ref[...] = jnp.zeros_like(best_ref)
        before = mask(iota((lanes, lanes), 0) < iota((lanes, lanes), 1))
        seen = jnp.zeros((8, 1), F32)
        for block in range(slots // lanes):
            here = pl.ds(block * lanes, lanes)
            ids = lists_ref[:, here]
            hit = mask(ids == iota((8, lanes), 0) + 1)
            hit32 = hit.astype(F32)
            rank = mm(hit, before) + seen
            seen = seen + jnp.sum(hit32, axis=1, keepdims=True)
            rank = jnp.sum(rank * hit32, axis=0, keepdims=True).astype(I32)
            bucket_ref[:, here] = jnp.where(ids > 0, (ids - 1) * per_list + rank, count * per_list)

    select = mask(iota((per_list, slots), 0) == bucket_ref[...] - which * per_list)
    grouped = mm(select, vec_ref[...]).astype(BF16)
    scores = mm(rows_ref[0], grouped, ROW)
    scores = jnp.where(iota(scores.shape, 0) < fill_ref[which], scores, -jnp.inf)
    best = jnp.max(scores, axis=0, keepdims=True)
    hi, mid, low = [term.astype(F32) for term in split(best)]
    part = iota((8, per_list), 0)
    parts = jnp.where(part == 0, hi, jnp.where(part == 1, mid, jnp.where(part == 2, low, 0.0)))
    best_ref[...] += jnp.sum(mm(parts.astype(BF16), select), axis=0, keepdims=True)


def append_kernel(ids_ref, vec_ref, centroids_ref, sums_ref, codes_ref, scales_ref, out_ref, *, slots):
    count = ids_ref.shape[1]
    lists = centroids_ref.shape[0]
    ids = ids_ref[...]
    hit = mask(ids == iota((lists, count), 0) + 1)
    before = mask(iota((count, count), 0) < iota((count, count), 1))
    rank = jnp.sum(mm(hit, before) * hit.astype(F32), axis=0, keepdims=True).astype(I32)
    slot = jnp.where(ids > 0, (ids - 1) * slots + rank, lists * slots)
    center = sum(mm(hit, term, COL) for term in split(centroids_ref[...]))
    residual = vec_ref[...].astype(F32) - center
    scale = jnp.max(jnp.abs(residual), axis=1, keepdims=True) + 1e-06
    place = mask(iota((lists * slots, count), 0) == slot)
    codes_ref[...] = mm(place, (residual / scale).astype(BF16)).astype(BF16)
    wide = jnp.broadcast_to(scale, (count, 128))
    scales_ref[...] = sum(mm(place, term) for term in split(wide))[:, :1]
    out_ref[...] = sums_ref[...] + sum(mm(hit, term) for term in split(residual))


def pick_kernel(probes_ref, rank_ref, best_ref, out_ref, *, list_count):
    group_size, cap = best_ref.shape
    probe_count = probes_ref.shape[1]
    lists = columns(probes_ref[...])
    rank = columns(rank_ref[...])
    hot = mask(lists // list_count == iota((lists.shape[0], group_size), 1))
    found = sum(mm(hot, term) for term in split(best_ref[...]))
    mine = jnp.where(rank == iota(found.shape, 1), found, 0.0)
    out_ref[...] = uncolumns(jnp.sum(mine, axis=1, keepdims=True), probe_count)


def vmem(count):
    return [pl.BlockSpec(memory_space=pltpu.VMEM)] * count


def shape(dims, dtype):
    return jax.ShapeDtypeStruct(dims, dtype)


def exchange(x):
    return lax.all_to_all(x, ("lr", "lc"), split_axis=0, concat_axis=0, tiled=True)


def local(queries, probes, assign, list_rows, list_fill, centroids, list_sums):
    group_size = lax.axis_size("lr") * lax.axis_size("lc")
    list_count, row_count, feature_dim = list_rows.shape
    query_count, probe_count = probes.shape
    cap = 2 * query_count * probe_count // group_size
    cap2 = max(2, 2 * query_count // group_size)
    per_list = group_size * cap // list_count
    append_slots = group_size * cap2 // list_count
    slots, slots2 = group_size * cap, group_size * cap2

    table, rank = pl.pallas_call(
        functools.partial(
            route_kernel, group_size=group_size, list_count=list_count, caps=(cap, cap2)
        ),
        out_shape=(shape((group_size, 128), F32), shape((query_count, probe_count), I32)),
        in_specs=vmem(2),
        out_specs=tuple(vmem(2)),
        name="route",
    )(probes, assign[:, None])
    table = table.astype(I32)
    ids = jnp.concatenate([table[:, cap : 2 * cap], table[:, 2 * cap + cap2 : 2 * cap + 2 * cap2]], axis=1)

    def pick(which):
        hot = (which[:, :, None] == jnp.arange(query_count, dtype=I32)).astype(BF16)
        hot = hot.reshape(-1, query_count)
        picked = jnp.dot(hot, queries, preferred_element_type=F32).astype(BF16)
        return picked.reshape(group_size, -1, feature_dim)

    ids = exchange(ids)
    new = exchange(pick(table[:, 2 * cap : 2 * cap + cap2]))
    vectors = exchange(pick(table[:, :cap]))

    best = pl.pallas_call(
        functools.partial(score_kernel, per_list=per_list),
        grid=(list_count,),
        out_shape=shape((1, slots), F32),
        in_specs=[
            pl.BlockSpec(memory_space=pltpu.SMEM),
            pl.BlockSpec((1, slots), lambda i: (0, 0)),
            pl.BlockSpec((slots, feature_dim), lambda i: (0, 0)),
            pl.BlockSpec((1, row_count, feature_dim), lambda i: (i, 0, 0)),
        ],
        out_specs=pl.BlockSpec((1, slots), lambda i: (0, 0)),
        scratch_shapes=[pltpu.VMEM((1, slots), I32)],
        compiler_params=pltpu.CompilerParams(
            dimension_semantics=("arbitrary",), vmem_limit_bytes=48 << 20
        ),
        name="score",
    )(list_fill, ids[:, :cap].reshape(1, slots), vectors.reshape(slots, feature_dim), list_rows)

    codes, scales, sums = pl.pallas_call(
        functools.partial(append_kernel, slots=append_slots),
        out_shape=(
            shape((slots2, feature_dim), BF16),
            shape((slots2, 1), F32),
            shape((list_count, feature_dim), F32),
        ),
        in_specs=vmem(4),
        out_specs=tuple(vmem(3)),
        name="append",
    )(ids[:, cap:].reshape(1, slots2), new.reshape(slots2, feature_dim), centroids, list_sums)

    maxima = exchange(best.reshape(group_size, cap))
    dup_max = pl.pallas_call(
        functools.partial(pick_kernel, list_count=list_count),
        out_shape=shape((query_count, probe_count), F32),
        in_specs=vmem(3),
        out_specs=pl.BlockSpec(memory_space=pltpu.VMEM),
        name="pick",
    )(probes, rank, maxima)
    return (
        dup_max,
        codes.reshape(list_count, append_slots, feature_dim),
        scales.reshape(list_count, append_slots),
        sums,
    )


def solution(mesh):
    rows = P(("lr", "lc"), None)
    return jax.shard_map(
        local,
        mesh=mesh,
        in_specs=(rows, rows, P(("lr", "lc")), P(("lr", "lc"), None, None), P(("lr", "lc")), rows, rows),
        out_specs=(rows, P(("lr", "lc"), None, None), rows, rows),
        check_vma=False,
    )
```

profile of v0, /device:TPU:1, one launch (start us, length us, event | category | flops | bytes accessed | tf_op | source)
XLA Modules:
  0.0 124.7 jit_solution(133440117633604860)
XLA Ops:
  0.6 1.4 %copy.31.probes_ref = s32[64,16]{1,0:T(8,128)} copy(s32[64,16]{0,1:T(8,128)} %param.8) | data formatting | bytes 8192 | tf_op args[1]
  2.1 1.4 %copy.28.assign_ref = s32[64,1]{1,0:T(8,128)} copy(s32[64,1]{0,1:T(1,128)} %bitcast.18) | data formatting | bytes 512 | tf_op jit(solution)/shard_map/broadcast_in_dim | solution.py:169
  3.4 2.8 %route.1 = (f32[128,128]{1,0:T(8,128)}, s32[64,16]{1,0:T(8,128)}) custom-call(s32[64,16]{1,0:T(8,128)} %copy.31.probes_ref, s32[64,1]{1,0:T(8,128)} %copy.28.assign_ref), custom_call_target="tpu_custom_call" | custom-call | tf_op jit(solution)/shard_map/route/pallas_call | solution.py:161
  6.2 0.8 convert_element_type.11
  7.2 0.7 pad_add_fusion
  7.9 11.5 %all-to-all-start = ((s32[128,1,18]{2,1,0:T(1,128)}), s32[128,1,18]{2,1,0:T(1,128)S(1)}, u32[]{:S(2)}, u32[]{:S(2)}) async-start(s32[128,1,18]{2,1,0:T(1,128)} %bitcast.2), calls=%async_computation | async-start | bytes 131072 | tf_op jit(solution)/shard_map/all_to_all | solution.py:148
  19.5 2.4 %convolution_convert_fusion = bf16[2048,768]{1,0:T(8,128)(2,1)} fusion(bf16[64,768]{1,0:T(8,128)(2,1)S(1)} %copy-done, s32[2048]{0:T(1024)S(1)} %eq.32), kind=kOutput, calls=%fused_computation | convolution fusion | flops 203030528 | bytes 3252224 | tf_op jit(solution)/shard_map/dot_general | solution.py:176
  21.9 6.8 %all-to-all-done = s32[128,1,18]{2,1,0:T(1,128)S(1)} async-done(((s32[128,1,18]{2,1,0:T(1,128)}), s32[128,1,18]{2,1,0:T(1,128)S(1)}, u32[]{:S(2)}, u32[]{:S(2)}) %all-to-all-start) | async-done | bytes 9248 | tf_op jit(solution)/shard_map/all_to_all | solution.py:148
  28.7 4.8 %all-to-all-start.1 = ((bf16[128,16,768]{2,1,0:T(8,128)(2,1)}), bf16[128,16,768]{2,1,0:T(8,128)(2,1)S(1)}, u32[]{:S(2)}, u32[]{:S(2)}) async-start(bf16[128,16,768]{2,1,0:T(8,128)(2,1)} %bitcast.14), calls=%async_computation.1 | async-start | bytes 6291456 | tf_op jit(solution)/shard_map/all_to_all | solution.py:148
  33.7 1.1 convolution_convert_fusion.1
  34.7 1.9 %reshape.50 = bf16[128,2,768]{2,1,0:T(2,128)(2,1)} reshape(bf16[256,768]{1,0:T(8,128)(2,1)} %convolution_convert_fusion.1) | data formatting | bytes 786432 | tf_op jit(solution)/shard_map/reshape | solution.py:177
  36.6 38.9 %all-to-all-done.1 = bf16[128,16,768]{2,1,0:T(8,128)(2,1)S(1)} async-done(((bf16[128,16,768]{2,1,0:T(8,128)(2,1)}), bf16[128,16,768]{2,1,0:T(8,128)(2,1)S(1)}, u32[]{:S(2)}, u32[]{:S(2)}) %all-to-all-start.1) | async-done | bytes 3145760 | tf_op jit(solution)/shard_map/all_to_all | solution.py:148
  75.5 5.4 %all-to-all-start.3 = ((bf16[128,2,768]{2,1,0:T(2,128)(2,1)}), bf16[128,2,768]{2,1,0:T(2,128)(2,1)}, u32[]{:S(2)}, u32[]{:S(2)}) async-start(bf16[128,2,768]{2,1,0:T(2,128)(2,1)} %reshape.50), calls=%async_computation.3 | async-start | bytes 786432 | tf_op jit(solution)/shard_map/all_to_all | solution.py:148
  81.1 18.1 %score.1 = f32[1,2048]{1,0:T(1,128)S(1)} custom-call(s32[8]{0:T(128)S(1)} %copy-done.1, s32[1,2048]{1,0:T(1,128)S(1)} %reshape.46.lists_ref, bf16[2048,768]{1,0:T(8,128)(2,1)S(1)} %bitcast.13, bf16[8,1024,768]{2,1,0:T(8,128)(2,1)} %rows_ref.1), custom_call_target="tpu_custom_call" | custom-call | tf_op jit(solution)/shard_map/score/pallas_call | solution.py:183
  100.3 0.7 all_to_all.25
  101.0 9.9 %all-to-all-start.2 = ((f32[128,1,16]{2,1,0:T(1,128)}), f32[128,1,16]{2,1,0:T(1,128)S(1)}, u32[]{:S(2)}, u32[]{:S(2)}) async-start(f32[128,1,16]{2,1,0:T(1,128)} %bitcast.6), calls=%async_computation.2 | async-start | bytes 131072 | tf_op jit(solution)/shard_map/all_to_all | solution.py:148
  111.0 0.7 reshape.49.ids_ref
  111.7 1.9 %reshape.51.vec_ref = bf16[256,768]{1,0:T(8,128)(2,1)} reshape(bf16[128,2,768]{2,1,0:T(2,128)(2,1)} %all-to-all-done.3) | data formatting | bytes 786432 | tf_op jit(solution)/shard_map/reshape | solution.py:211
  113.6 2.9 %append.1 = (bf16[256,768]{1,0:T(8,128)(2,1)}, f32[256,1]{1,0:T(8,128)}, f32[8,768]{1,0:T(8,128)}) custom-call(s32[1,256]{1,0:T(1,128)} %reshape.49.ids_ref, bf16[256,768]{1,0:T(8,128)(2,1)} %reshape.51.vec_ref, f32[8,768]{1,0:T(8,128)} %centroids_ref.1, f32[8,768]{1,0:T(8,128)} %sums_ref.1), custom_call_target="tpu_custom_call" | custom-call | tf_op jit(solution)/shard_map/append/pallas_call | solution.py:201
  116.5 1.0 reduce.1
  117.5 0.7 reshape.53
  118.2 2.1 %all-to-all-done.2 = f32[128,1,16]{2,1,0:T(1,128)S(1)} async-done(((f32[128,1,16]{2,1,0:T(1,128)}), f32[128,1,16]{2,1,0:T(1,128)S(1)}, u32[]{:S(2)}, u32[]{:S(2)}) %all-to-all-start.2) | async-done | bytes 8224 | tf_op jit(solution)/shard_map/all_to_all | solution.py:148
  120.9 2.3 %pick.1 = f32[64,16]{1,0:T(8,128)} custom-call(s32[64,16]{1,0:T(8,128)} %copy.31.probes_ref, s32[64,16]{1,0:T(8,128)} %get-tuple-element.9.rank_ref, f32[128,16]{1,0:T(8,128)} %bitcast.17), custom_call_target="tpu_custom_call" | custom-call | tf_op jit(solution)/shard_map/pick/pallas_call | solution.py:214
  123.2 1.4 %copy.32 = f32[64,16]{0,1:T(8,128)} copy(f32[64,16]{1,0:T(8,128)} %pick.1) | data formatting | bytes 8192
  (15 shorter events, 2.4 us)
Async XLA Ops:
  0.6 18.9 %copy-start = (bf16[64,768]{1,0:T(8,128)(2,1)S(1)}, bf16[64,768]{1,0:T(8,128)(2,1)}, u32[]{:S(2)}) copy-start(bf16[64,768]{1,0:T(8,128)(2,1)} %param.7) | copy-start | bytes 294916
  7.9 20.8 %all-to-all-start = ((s32[128,1,18]{2,1,0:T(1,128)}), s32[128,1,18]{2,1,0:T(1,128)S(1)}, u32[]{:S(2)}, u32[]{:S(2)}) async-start(s32[128,1,18]{2,1,0:T(1,128)} %bitcast.2), calls=%async_computation | async-start | bytes 131072 | tf_op jit(solution)/shard_map/all_to_all | solution.py:148
  28.7 52.3 %copy-start.1 = (s32[8]{0:T(128)S(1)}, s32[8]{0:T(128)}, u32[]{:S(2)}) copy-start(s32[8]{0:T(128)} %fill_ref.1) | copy-start | bytes 100
  28.7 46.8 %all-to-all-start.1 = ((bf16[128,16,768]{2,1,0:T(8,128)(2,1)}), bf16[128,16,768]{2,1,0:T(8,128)(2,1)S(1)}, u32[]{:S(2)}, u32[]{:S(2)}) async-start(bf16[128,16,768]{2,1,0:T(8,128)(2,1)} %bitcast.14), calls=%async_computation.1 | async-start | bytes 6291456 | tf_op jit(solution)/shard_map/all_to_all | solution.py:148
  75.5 25.5 %all-to-all-start.3 = ((bf16[128,2,768]{2,1,0:T(2,128)(2,1)}), bf16[128,2,768]{2,1,0:T(2,128)(2,1)}, u32[]{:S(2)}, u32[]{:S(2)}) async-start(bf16[128,2,768]{2,1,0:T(2,128)(2,1)} %reshape.50), calls=%async_computation.3 | async-start | bytes 786432 | tf_op jit(solution)/shard_map/all_to_all | solution.py:148
  101.0 19.3 %all-to-all-start.2 = ((f32[128,1,16]{2,1,0:T(1,128)}), f32[128,1,16]{2,1,0:T(1,128)S(1)}, u32[]{:S(2)}, u32[]{:S(2)}) async-start(f32[128,1,16]{2,1,0:T(1,128)} %bitcast.6), calls=%async_computation.2 | async-start | bytes 131072 | tf_op jit(solution)/shard_map/all_to_all | solution.py:148
  120.3 0.6 copy-start.2
where the time goes:
time: 125 us
  waiting for transfers between devices  47.8 us (38%)
  starting transfers between devices  31.6 us (25%)
  Pallas kernels  26 us (21%)
  local copies, waits for them, and re-layouts  11.8 us (9%)
  matrix products  3.49 us (3%)
  other arithmetic  3.25 us (3%)
    all_to_all x4, waiting for transfers between devices, exchange(): lax.all_to_all(x, ('lr', 'lc'), split_axis=0, concat_axis=0, tiled=True)  47.8 us
    all_to_all x4, starting transfers between devices, exchange(): lax.all_to_all(x, ('lr', 'lc'), split_axis=0, concat_axis=0, tiled=True)  31.6 us
    pallas_call x1, Pallas kernels, local(): pl.pallas_call(functools.partial(score_kernel, per_list=per_list), grid=(...  18.1 us
    dot_general x2, matrix products, pick(): picked = jnp.dot(hot, queries, preferred_element_type=F32).astype(BF16)  3.49 us
    unnamed x8, local copies, waits for them, and re-layouts  3.47 us
    pallas_call x1, Pallas kernels, local(): pl.pallas_call(functools.partial(append_kernel, slots=append_slots), out_...  2.86 us
    pallas_call x1, Pallas kernels, local(): pl.pallas_call(functools.partial(route_kernel, group_size=group_size, lis...  2.75 us
  transfers between devices with their start and end apart: 4, of which 3 were waited for; matrix products, arithmetic and copies ran while one was open for 9% of the time, Pallas kernels for 17%

commit v1 on v0

v1 whole, which is shorter than its diff:
```python
import functools

import jax
import jax.numpy as jnp
from jax import lax
from jax.experimental import pallas as pl
from jax.experimental.pallas import tpu as pltpu
from jax.sharding import PartitionSpec as P

BF16, F32, I32 = jnp.bfloat16, jnp.float32, jnp.int32
ROW = (((1,), (1,)), ((), ()))
COL = (((0,), (0,)), ((), ()))
SIDE = 4
MESH = pl.DeviceIdType.MESH
GROUPS = 8


def iota(shape, axis):
    return lax.broadcasted_iota(I32, shape, axis)


def mask(cond):
    return jnp.where(cond, 1.0, 0.0).astype(BF16)


def mm(a, b, dims=(((1,), (0,)), ((), ()))):
    return lax.dot_general(a, b, dims, preferred_element_type=F32)


def split(x):
    hi = x.astype(BF16)
    rest = x - hi.astype(F32)
    mid = rest.astype(BF16)
    return hi, mid, (rest - mid.astype(F32)).astype(BF16)


def columns(table):
    return jnp.concatenate([table[:, j : j + 1] for j in range(table.shape[1])], axis=0)


def uncolumns(column, count):
    rows = column.shape[0] // count
    lane = iota((rows, count), 1)
    out = jnp.zeros((rows, count), column.dtype)
    for j in range(count):
        out = jnp.where(lane == j, column[j * rows : (j + 1) * rows], out)
    return out


def rank_by_owner(owners, group_size):
    count = owners.shape[0]
    hot = mask(owners == iota((count, group_size), 1))
    earlier = mask(iota((count, count), 1) < iota((count, count), 0))
    before = mm(earlier, hot)
    rank = jnp.sum(before * hot.astype(F32), axis=1, keepdims=True).astype(I32)
    return hot, rank


def step_of(owner, me):
    x, y, z, c = me
    dx = (owner // 32 + SIDE - x) % SIDE
    dy = (owner // 8 + SIDE - y) % SIDE
    dz = (owner // 2 + SIDE - z) % SIDE
    dc = (owner + 2 - c) % 2
    return ((dz + SIDE - dx) % SIDE * 16 + (dy + SIDE - dx) % SIDE * 4 + dx) * 2 + dc


def offset_of(step):
    dx = step // 2 % SIDE
    return dx, (step // 8 + dx) % SIDE, (step // 32 + dx) % SIDE, step % 2


def position():
    lr, lc = lax.axis_index("lr"), lax.axis_index("lc")
    return lr // SIDE, lr % SIDE, lc // 2, lc % 2


def device(me, offset):
    x, y, z, c = [(own + far) % side for own, far, side in zip(me, offset, (SIDE, SIDE, SIDE, 2))]
    return x * SIDE + y, z * 2 + c


def route_kernel(probes_ref, assign_ref, table_ref, rank_ref, *, group_size, list_count, caps):
    cap, cap2 = caps
    me = position()
    query_count, probe_count = probes_ref.shape
    probes = probes_ref[...]
    pair_count = query_count * probe_count
    hot, rank = rank_by_owner(columns(step_of(probes // list_count, me)), group_size)
    rank_ref[...] = uncolumns(rank, probe_count)
    lane = iota((pair_count, 128), 1)
    query = columns(iota((query_count, probe_count), 0)).astype(F32)
    place = columns(probes % list_count + 1).astype(F32)
    values = jnp.where(lane == rank, query, 0.0) + jnp.where(lane == rank + cap, place, 0.0)
    table = mm(hot, values.astype(BF16), COL)

    ids = assign_ref[...]
    hot2, rank2 = rank_by_owner(step_of(ids // list_count, me), group_size)
    lane2 = iota((query_count, 128), 1) - 2 * cap
    query2 = iota((query_count, 1), 0).astype(F32)
    place2 = (ids % list_count + 1).astype(F32)
    values2 = jnp.where(lane2 == rank2, query2, 0.0) + jnp.where(lane2 == rank2 + cap2, place2, 0.0)
    table_ref[...] = table + mm(hot2, values2.astype(BF16), COL)


def arrival_order(slot, count):
    dx, dy, dz, dc = offset_of(slot % count)
    x, y, z, c = position()
    sx, sy, sz = [(own + SIDE - far) % SIDE for own, far in ((x, dx), (y, dy), (z, dz))]
    return (((sx * SIDE + sy) * SIDE + sz) * 2 + (c + 2 - dc) % 2) * 2 + slot // count


def append(ids, vectors, step_count, centroids, sums, codes_ref, scales_ref, out_ref):
    count = ids.shape[1]
    lists, slots = scales_ref.shape
    hit = mask(ids == iota((lists, count), 0) + 1)
    before = mask(arrival_order(iota((count, 1), 0), step_count) < arrival_order(iota((1, count), 1), step_count))
    rank = jnp.sum(mm(hit, before) * hit.astype(F32), axis=0, keepdims=True).astype(I32)
    slot = jnp.where(ids > 0, (ids - 1) * slots + rank, lists * slots)
    center = sum(mm(hit, term, COL) for term in split(centroids))
    residual = vectors.astype(F32) - center
    scale = jnp.max(jnp.abs(residual), axis=1, keepdims=True) + 1e-06
    place = mask(iota((lists * slots, count), 0) == slot)
    codes_ref[...] = mm(place, (residual / scale).astype(BF16)).astype(BF16)
    wide = jnp.broadcast_to(scale, (count, 128))
    placed = sum(mm(place, term) for term in split(wide))
    placed = jnp.where(iota((lists * slots, 1), 0) % slots == iota((1, 128), 1), placed, 0.0)
    block = mask(iota((lists, 1), 0) == iota((1, lists * slots), 1) // slots)
    scales_ref[...] = sum(mm(block, term) for term in split(placed))[:, :slots]
    out_ref[...] = sums + sum(mm(hit, term) for term in split(residual))


def pick(probes_ref, rank_ref, best, out_ref, list_count):
    group_size, cap = best.shape
    probe_count = probes_ref.shape[1]
    steps = columns(step_of(probes_ref[...] // list_count, position()))
    rank = columns(rank_ref[...])
    hot = mask(steps == iota((steps.shape[0], group_size), 1))
    found = sum(mm(hot, term) for term in split(best))
    mine = jnp.where(rank == iota(found.shape, 1), found, 0.0)
    out_ref[...] = uncolumns(jnp.sum(mine, axis=1, keepdims=True), probe_count)


def vmem(count):
    return [pl.BlockSpec(memory_space=pltpu.VMEM)] * count


def shape(dims, dtype):
    return jax.ShapeDtypeStruct(dims, dtype)


def routes(me):
    x, y, z, c = me
    xs, ys, zs = [[(own + far) % SIDE for far in range(SIDE)] for own in (x, y, z)]
    cores = [c, 1 - c]
    rows = [[xs[i] * SIDE + ys[j] for j in range(SIDE)] for i in range(SIDE)]
    cols = [[zs[k] * 2 + cores[l] for l in range(2)] for k in range(SIDE)]
    return lambda far: (rows[far[0]][far[1]], cols[far[2]][far[3]])


def greet(to, count):
    barrier = pltpu.get_barrier_semaphore()
    for step in range(1, count):
        pl.semaphore_signal(barrier, inc=1, device_id=to(offset_of(step)), device_id_type=MESH)
    pl.semaphore_wait(barrier, count - 1)


def buckets(lists, list_count, per_list):
    slots, lanes = lists.shape[1], 128
    before = mask(iota((lanes, lanes), 0) < iota((lanes, lanes), 1))
    seen = jnp.zeros((list_count, 1), F32)
    out = []
    for block in range(slots // lanes):
        ids = lists[:, block * lanes : (block + 1) * lanes]
        hit = mask(ids == iota((list_count, lanes), 0) + 1)
        hit32 = hit.astype(F32)
        rank = mm(hit, before) + seen
        seen = seen + jnp.sum(hit32, axis=1, keepdims=True)
        rank = jnp.sum(rank * hit32, axis=0, keepdims=True).astype(I32)
        out.append(jnp.where(ids > 0, (ids - 1) * per_list + rank, list_count * per_list))
    return jnp.concatenate(out, axis=1)


def ingest_kernel(
    fill_ref, probes_ref, rank_ref, ids_ref, new_ref, vec_ref, rows_ref, centroids_ref, sums_ref,
    dup_ref, codes_ref, scales_ref, out_ref,
    got_ids, got_new, got_vec, best_ref, got_best, rows, grouped, bucket_ref, row_ref,
    small_sem, vec_send, vec_recv, back_sem, rows_sem, own_sem,
    *, per_list,
):
    count, cap, feature_dim = vec_ref.shape
    list_count = rows_ref.shape[0]
    slots = count * cap
    each = count // GROUPS
    to = routes(position())
    steps = range(1, count)
    every = pl.ds(1, count - 1)
    near = (0, 0, 0, 1)

    def exchange(src, dst, send, recv, where, far):
        return pltpu.make_async_remote_copy(
            src_ref=src.at[where], dst_ref=dst.at[where], send_sem=send, recv_sem=recv,
            device_id=to(far), device_id_type=MESH,
        )

    def rows_copy(which):
        return pltpu.make_async_copy(rows_ref.at[which], rows.at[which], rows_sem.at[which])

    def own_copy(src, dst, i):
        return pltpu.make_async_copy(src.at[0], dst.at[0], own_sem.at[i])

    own = [own_copy(src, dst, i) for i, (src, dst) in enumerate(((ids_ref, got_ids), (new_ref, got_new), (vec_ref, got_vec)))]
    for copy in own:
        copy.start()
    for which in range(list_count):
        rows_copy(which).start()
    greet(to, count)
    for step in steps:
        exchange(ids_ref, got_ids, small_sem.at[0], small_sem.at[1], step, offset_of(step)).start()
    for step in steps:
        exchange(vec_ref, got_vec, vec_send, vec_recv.at[step // each], step, offset_of(step)).start()
        exchange(new_ref, got_new, small_sem.at[2], small_sem.at[3], step, offset_of(step)).start()

    grouped[...] = jnp.zeros_like(grouped)
    for copy in own:
        copy.wait()
    exchange(ids_ref, got_ids, small_sem.at[0], small_sem.at[1], every, near).wait()
    ids = got_ids[:, 0, :].astype(F32).T
    spread = mm(ids[:cap].astype(BF16), mask(iota((count, 1), 0) == iota((1, slots), 1) // cap))
    lists = jnp.where(iota((cap, 1), 0) == iota((1, slots), 1) % cap, spread, 0.0)
    lists = jnp.sum(lists, axis=0, keepdims=True).astype(I32)
    bucket_ref[...] = buckets(lists, list_count, per_list)

    for group in range(GROUPS):
        first = max(1, group * each)
        part = pl.ds(first, (group + 1) * each - first)
        exchange(vec_ref, got_vec, vec_send, vec_recv.at[group], part, near).wait_recv()
        bucket = bucket_ref[:, group * each * cap : (group + 1) * each * cap]

        @pl.loop(0, list_count)
        def _(which):
            here = pl.ds(pl.multiple_of(which * per_list, per_list), per_list)
            select = mask(iota((per_list, each * cap), 0) == bucket - which * per_list)
            vectors = got_vec[group * each : (group + 1) * each].reshape(each * cap, feature_dim)
            grouped[here] += mm(select, vectors).astype(BF16)

    row_ref[...] = jnp.zeros_like(row_ref)

    @pl.loop(0, list_count)
    def _(which):
        rows_copy(which).wait()
        here = pl.ds(pl.multiple_of(which * per_list, per_list), per_list)
        scores = mm(rows[which], grouped[here], ROW)
        scores = jnp.where(iota(scores.shape, 0) < fill_ref[which], scores, -jnp.inf)
        best = jnp.max(scores, axis=0, keepdims=True)
        hi, mid, low = [term.astype(F32) for term in split(best)]
        part = iota((8, per_list), 0)
        parts = jnp.where(part == 0, hi, jnp.where(part == 1, mid, jnp.where(part == 2, low, 0.0)))
        select = mask(iota((per_list, slots), 0) == bucket_ref[...] - which * per_list)
        row_ref[...] += jnp.sum(mm(parts.astype(BF16), select), axis=0, keepdims=True)

    mine = jnp.where(iota((cap, 1), 0) == iota((1, slots), 1) % cap, row_ref[...], 0.0)
    spot = mask(iota((count, 1), 0) == iota((1, slots), 1) // cap)
    best = sum(mm(term, spot, ROW) for term in split(mine))
    best = jnp.concatenate([best, jnp.zeros((128 - cap, count), F32)], axis=0)
    best_ref[...] = best.T[:, None, :]
    back_own = own_copy(best_ref, got_best, 0)
    back_own.start()
    for step in steps:
        far = offset_of(step)
        back = tuple((SIDE - d) % SIDE for d in far[:3]) + (far[3],)
        exchange(best_ref, got_best, back_sem.at[0], back_sem.at[1], step, back).start()

    exchange(new_ref, got_new, small_sem.at[2], small_sem.at[3], every, near).wait()
    exchange(vec_ref, got_vec, vec_send, vec_recv.at[0], every, near).wait_send()
    vectors = jnp.concatenate([got_new[:, k, :] for k in range(2)], axis=0)
    new_ids = jnp.concatenate([ids[cap + 2 + k : cap + 3 + k] for k in range(2)], axis=1).astype(I32)
    append(new_ids, vectors, count, centroids_ref[...], sums_ref[...], codes_ref, scales_ref, out_ref)
    back_own.wait()
    exchange(best_ref, got_best, back_sem.at[0], back_sem.at[1], every, near).wait()
    pick(probes_ref, rank_ref, got_best[:, 0, :cap], dup_ref, list_count)


def local(queries, probes, assign, list_rows, list_fill, centroids, list_sums):
    group_size = lax.axis_size("lr") * lax.axis_size("lc")
    list_count, row_count, feature_dim = list_rows.shape
    query_count, probe_count = probes.shape
    cap = 2 * query_count * probe_count // group_size
    cap2 = max(2, 2 * query_count // group_size)
    per_list = group_size * cap // list_count
    append_slots = group_size * cap2 // list_count
    slots, slots2 = group_size * cap, group_size * cap2

    table, rank = pl.pallas_call(
        functools.partial(
            route_kernel, group_size=group_size, list_count=list_count, caps=(cap, cap2)
        ),
        out_shape=(shape((group_size, 128), F32), shape((query_count, probe_count), I32)),
        in_specs=vmem(2),
        out_specs=tuple(vmem(2)),
        name="route",
    )(probes, assign[:, None])
    table = table.astype(I32)
    ids = jnp.pad(table[:, cap : 2 * cap + 2 * cap2], ((0, 0), (0, 128 - cap - 2 * cap2)))[:, None, :]

    def chosen(which):
        hot = (which[:, :, None] == jnp.arange(query_count, dtype=I32)).astype(BF16)
        hot = hot.reshape(-1, query_count)
        picked = jnp.dot(hot, queries, preferred_element_type=F32).astype(BF16)
        return picked.reshape(group_size, -1, feature_dim)

    buffers = [
        pltpu.VMEM((group_size, 1, 128), I32),
        pltpu.VMEM((group_size, cap2, feature_dim), BF16),
        pltpu.VMEM((group_size, cap, feature_dim), BF16),
        pltpu.VMEM((group_size, 1, 128), F32),
        pltpu.VMEM((group_size, 1, 128), F32),
        pltpu.VMEM((list_count, row_count, feature_dim), BF16),
        pltpu.VMEM((slots, feature_dim), BF16),
        pltpu.VMEM((1, slots), I32),
        pltpu.VMEM((1, slots), F32),
    ]
    DMA = pltpu.SemaphoreType.DMA
    dup_max, codes, scales, sums = pl.pallas_call(
        functools.partial(ingest_kernel, per_list=per_list),
        out_shape=(
            shape((query_count, probe_count), F32),
            shape((slots2, feature_dim), BF16),
            shape((list_count, append_slots), F32),
            shape((list_count, feature_dim), F32),
        ),
        in_specs=[
            pl.BlockSpec(memory_space=pltpu.SMEM),
            *vmem(5),
            pl.BlockSpec(memory_space=pl.ANY),
            *vmem(2),
        ],
        out_specs=tuple(vmem(4)),
        scratch_shapes=buffers
        + [DMA((4,)), DMA, DMA((GROUPS,)), DMA((2,)), DMA((list_count,)), DMA((3,))],
        compiler_params=pltpu.CompilerParams(
            collective_id=0, has_side_effects=True, vmem_limit_bytes=58 << 20
        ),
        name="ingest",
    )(
        list_fill, probes, rank, ids, chosen(table[:, 2 * cap : 2 * cap + cap2]),
        chosen(table[:, :cap]), list_rows, centroids, list_sums,
    )
    return dup_max, codes.reshape(list_count, append_slots, feature_dim), scales, sums


def solution(mesh):
    rows = P(("lr", "lc"), None)
    return jax.shard_map(
        local,
        mesh=mesh,
        in_specs=(rows, rows, P(("lr", "lc")), P(("lr", "lc"), None, None), P(("lr", "lc")), rows, rows),
        out_specs=(rows, P(("lr", "lc"), None, None), rows, rows),
        check_vma=False,
    )
```

time: 125 us -> 99.4 us (0.80)
  Pallas kernels: 26 us -> 84.2 us
  waiting for transfers between devices: 47.8 us -> 0 us
  starting transfers between devices: 31.6 us -> 0 us
  other arithmetic: 3.25 us -> 0.85 us
  local copies, waits for them, and re-layouts: 11.8 us -> 10.5 us
    pallas_call x3 -> x1, Pallas kernels: 23.2 us -> 81.1 us  [local(): pl.pallas_call(functools.partial(ingest_kernel, per_list=per_list), out_s...]
    all_to_all x4 -> x0, waiting for transfers between devices: 47.8 us -> none  [exchange(): lax.all_to_all(x, ('lr', 'lc'), split_axis=0, concat_axis=0, tiled=True)]
    all_to_all x4 -> x0, starting transfers between devices: 31.6 us -> none  [exchange(): lax.all_to_all(x, ('lr', 'lc'), split_axis=0, concat_axis=0, tiled=True)]
    reshape x5 -> x1, local copies, waits for them, and re-layouts: 5.25 us -> 0.9 us  [chosen(): return picked.reshape(group_size, -1, feature_dim)]
    unnamed x8 -> x7, local copies, waits for them, and re-layouts: 3.47 us -> 7.24 us
    pallas_call x2 -> x0, other arithmetic: 1.67 us -> none  [the longest x1 1.01 us: local(): pl.pallas_call(functools.partial(append_kernel, slots=append_slots), out_...]
  transfers between devices with their start and end apart: 4 -> 0, of which waited for: 3 -> 0; matrix products, arithmetic and copies ran while one was open for 9% -> 0% of each run, Pallas kernels for 17% -> 0%
where the time goes in v1:
time: 99.4 us; the launch traced here: 98.9 us
  Pallas kernels  84.2 us (85%)
  local copies, waits for them, and re-layouts  10.5 us (11%)
  matrix products  2.73 us (3%)
    pallas_call x1, Pallas kernels, local(): pl.pallas_call(functools.partial(ingest_kernel, per_list=per_list), out_s...  81.1 us
    unnamed x7, local copies, waits for them, and re-layouts  7.24 us
    pallas_call x1, Pallas kernels, local(): pl.pallas_call(functools.partial(route_kernel, group_size=group_size, lis...  3.04 us
    dot_general x2, matrix products, chosen(): picked = jnp.dot(hot, queries, preferred_element_type=F32).astype(BF16)  2.73 us

profile of v1, /device:TPU:1, one launch (start us, length us, event | category | flops | bytes accessed | tf_op | source)
XLA Modules:
  0.0 98.9 jit_solution(1322011059947124390)
XLA Ops:
  0.6 0.0 copy-start
  0.6 1.4 %copy.17.probes_ref = s32[64,16]{1,0:T(8,128)} copy(s32[64,16]{0,1:T(8,128)} %param.8) | data formatting | bytes 8192 | tf_op args[1]
  2.1 1.4 %copy.16.assign_ref = s32[64,1]{1,0:T(8,128)} copy(s32[64,1]{0,1:T(1,128)} %bitcast.11) | data formatting | bytes 512 | tf_op jit(solution)/shard_map/broadcast_in_dim | solution.py:302
  3.4 3.0 %route.1 = (f32[128,128]{1,0:T(8,128)}, s32[64,16]{1,0:T(8,128)}) custom-call(s32[64,16]{1,0:T(8,128)} %copy.17.probes_ref, s32[64,1]{1,0:T(8,128)} %copy.16.assign_ref), custom_call_target="tpu_custom_call" | custom-call | tf_op jit(solution)/shard_map/route/pallas_call | solution.py:294
  6.5 0.8 convert_element_type.11
  7.3 0.1 eq.36
  7.4 0.1 slice.13
  7.5 0.2 eq.32
  7.6 0.1 slice.12
  7.7 0.6 pad.4
  8.3 0.0 copy-done
  8.3 0.3 convolution_convert_fusion.1
  8.6 0.9 reshape.25.new_ref
  9.5 2.4 %convolution_convert_fusion = bf16[2048,768]{1,0:T(8,128)(2,1)} fusion(bf16[64,768]{1,0:T(8,128)(2,1)S(1)} %copy-done, s32[2048]{0:T(1024)S(1)} %eq.36), kind=kOutput, calls=%fused_computation | convolution fusion | flops 203030528 | bytes 3252224 | tf_op jit(solution)/shard_map/dot_general | solution.py:309
  12.0 81.1 %ingest.1 = (f32[64,16]{1,0:T(8,128)}, bf16[256,768]{1,0:T(8,128)(2,1)}, f32[8,32]{1,0:T(8,128)}, f32[8,768]{1,0:T(8,128)}) custom-call(s32[8]{0:T(128)} %fill_ref.1, s32[64,16]{1,0:T(8,128)} %copy.17.probes_ref, s32[64,16]{1,0:T(8,128)} %get-tuple-element.10.rank_ref, s32[128,1,128]{2,1,0:T(1,128)} %bitcast.10, bf16[128,2,768]{2,1,0:T(2,128)(2,1)} %reshape.25.new_ref, ...), custom_call_target="tpu_custom_call" | custom-call | tf_op jit(solution)/shard_map/ingest/pallas_call | solution.py:324
  93.1 1.4 %copy.18 = f32[64,16]{0,1:T(8,128)} copy(f32[64,16]{1,0:T(8,128)} %get-tuple-element.20) | data formatting | bytes 8192
  94.5 1.8 %copy.22 = bf16[8,32,768]{2,1,0:T(8,128)(2,1)} copy(bf16[8,32,768]{2,1,0:T(8,128)(2,1)} %bitcast.9) | data formatting | bytes 786432
  96.3 1.3 %copy.23 = f32[8,32]{1,0:T(8,128)} copy(f32[8,32]{1,0:T(8,128)} %get-tuple-element.30) | data formatting | bytes 2048
  97.6 1.3 %copy.24 = f32[8,768]{1,0:T(8,128)} copy(f32[8,768]{1,0:T(8,128)} %get-tuple-element.31) | data formatting | bytes 49152
Async XLA Ops:
  0.6 7.7 %copy-start = (bf16[64,768]{1,0:T(8,128)(2,1)S(1)}, bf16[64,768]{1,0:T(8,128)(2,1)}, u32[]{:S(2)}) copy-start(bf16[64,768]{1,0:T(8,128)(2,1)} %param.7) | copy-start | bytes 294916

commit v2 on v1

--- a/solution.py
+++ b/solution.py
@@ -34,17 +34,21 @@
     return hi, mid, (rest - mid.astype(F32)).astype(BF16)
 
 
+def eye(count):
+    return iota((count, count), 0) == iota((count, count), 1)
+
+
 def columns(table):
-    return jnp.concatenate([table[:, j : j + 1] for j in range(table.shape[1])], axis=0)
+    own = eye(table.shape[1])
+    turned = [jnp.where(own, table[j : j + 1], 0.0) for j in range(table.shape[0])]
+    return jnp.concatenate([jnp.sum(one, axis=1, keepdims=True) for one in turned], axis=0)
 
 
 def uncolumns(column, count):
-    rows = column.shape[0] // count
-    lane = iota((rows, count), 1)
-    out = jnp.zeros((rows, count), column.dtype)
-    for j in range(count):
-        out = jnp.where(lane == j, column[j * rows : (j + 1) * rows], out)
-    return out
+    size = column.shape[0] // count
+    own = eye(size)
+    turned = [jnp.where(own, column[j * size : (j + 1) * size], 0.0) for j in range(count)]
+    return jnp.concatenate([jnp.sum(one, axis=0, keepdims=True) for one in turned], axis=0)
 
 
 def rank_by_owner(owners, group_size):
@@ -80,27 +84,29 @@
     return x * SIDE + y, z * 2 + c
 
 
-def route_kernel(probes_ref, assign_ref, table_ref, rank_ref, *, group_size, list_count, caps):
+def route_kernel(probes_ref, assign_ref, table_ref, ids_ref, rank_ref, *, group_size, list_count, caps):
     cap, cap2 = caps
     me = position()
-    query_count, probe_count = probes_ref.shape
+    probe_count, query_count = probes_ref.shape
     probes = probes_ref[...]
     pair_count = query_count * probe_count
-    hot, rank = rank_by_owner(columns(step_of(probes // list_count, me)), group_size)
-    rank_ref[...] = uncolumns(rank, probe_count)
+    hot, rank = rank_by_owner(columns(step_of(probes // list_count, me).astype(F32)).astype(I32), group_size)
+    rank_ref[...] = uncolumns(rank.astype(F32), probe_count)
     lane = iota((pair_count, 128), 1)
-    query = columns(iota((query_count, probe_count), 0)).astype(F32)
-    place = columns(probes % list_count + 1).astype(F32)
+    query = columns(iota((probe_count, query_count), 1).astype(F32))
+    place = columns((probes % list_count + 1).astype(F32))
     values = jnp.where(lane == rank, query, 0.0) + jnp.where(lane == rank + cap, place, 0.0)
     table = mm(hot, values.astype(BF16), COL)
 
-    ids = assign_ref[...]
+    ids = columns(assign_ref[...].astype(F32)).astype(I32)
     hot2, rank2 = rank_by_owner(step_of(ids // list_count, me), group_size)
     lane2 = iota((query_count, 128), 1) - 2 * cap
     query2 = iota((query_count, 1), 0).astype(F32)
     place2 = (ids % list_count + 1).astype(F32)
     values2 = jnp.where(lane2 == rank2, query2, 0.0) + jnp.where(lane2 == rank2 + cap2, place2, 0.0)
-    table_ref[...] = table + mm(hot2, values2.astype(BF16), COL)
+    table = (table + mm(hot2, values2.astype(BF16), COL)).astype(I32)
+    table_ref[...] = table
+    ids_ref[...] = table[:, None, :]
 
 
 def arrival_order(slot, count):
@@ -130,15 +136,15 @@
     out_ref[...] = sums + sum(mm(hit, term) for term in split(residual))
 
 
-def pick(probes_ref, rank_ref, best, out_ref, list_count):
-    group_size, cap = best.shape
-    probe_count = probes_ref.shape[1]
-    steps = columns(step_of(probes_ref[...] // list_count, position()))
-    rank = columns(rank_ref[...])
-    hot = mask(steps == iota((steps.shape[0], group_size), 1))
+def finish_kernel(probes_ref, rank_ref, best_ref, codes_ref, scales_ref, sums_ref, dup_ref, *outs, list_count, cap):
+    best = best_ref[:, :cap]
+    steps = columns(step_of(probes_ref[...] // list_count, position()).astype(F32)).astype(I32)
+    hot = mask(steps == iota((steps.shape[0], best.shape[0]), 1))
     found = sum(mm(hot, term) for term in split(best))
-    mine = jnp.where(rank == iota(found.shape, 1), found, 0.0)
-    out_ref[...] = uncolumns(jnp.sum(mine, axis=1, keepdims=True), probe_count)
+    mine = jnp.where(columns(rank_ref[...]) == iota(found.shape, 1).astype(F32), found, 0.0)
+    dup_ref[...] = uncolumns(jnp.sum(mine, axis=1, keepdims=True), probes_ref.shape[0])
+    for src, dst in zip((codes_ref, scales_ref, sums_ref), outs):
+        dst[...] = src[...]
 
 
 def vmem(count):
@@ -182,9 +188,9 @@
 
 
 def ingest_kernel(
-    fill_ref, probes_ref, rank_ref, ids_ref, new_ref, vec_ref, rows_ref, centroids_ref, sums_ref,
-    dup_ref, codes_ref, scales_ref, out_ref,
-    got_ids, got_new, got_vec, best_ref, got_best, rows, grouped, bucket_ref, row_ref,
+    fill_ref, ids_ref, new_ref, vec_ref, rows_ref, centroids_ref, sums_ref,
+    max_ref, codes_ref, scales_ref, out_ref,
+    got_ids, got_new, got_vec, best_ref, got_best, rows, grouped, bucket_ref, bests_ref,
     small_sem, vec_send, vec_recv, back_sem, rows_sem, own_sem,
     *, per_list,
 ):
@@ -219,6 +225,7 @@
         exchange(ids_ref, got_ids, small_sem.at[0], small_sem.at[1], step, offset_of(step)).start()
     for step in steps:
         exchange(vec_ref, got_vec, vec_send, vec_recv.at[step // each], step, offset_of(step)).start()
+    for step in steps:
         exchange(new_ref, got_new, small_sem.at[2], small_sem.at[3], step, offset_of(step)).start()
 
     grouped[...] = jnp.zeros_like(grouped)
@@ -226,7 +233,7 @@
         copy.wait()
     exchange(ids_ref, got_ids, small_sem.at[0], small_sem.at[1], every, near).wait()
     ids = got_ids[:, 0, :].astype(F32).T
-    spread = mm(ids[:cap].astype(BF16), mask(iota((count, 1), 0) == iota((1, slots), 1) // cap))
+    spread = mm(ids[cap : 2 * cap].astype(BF16), mask(iota((count, 1), 0) == iota((1, slots), 1) // cap))
     lists = jnp.where(iota((cap, 1), 0) == iota((1, slots), 1) % cap, spread, 0.0)
     lists = jnp.sum(lists, axis=0, keepdims=True).astype(I32)
     bucket_ref[...] = buckets(lists, list_count, per_list)
@@ -244,22 +251,21 @@
             vectors = got_vec[group * each : (group + 1) * each].reshape(each * cap, feature_dim)
             grouped[here] += mm(select, vectors).astype(BF16)
 
-    row_ref[...] = jnp.zeros_like(row_ref)
-
     @pl.loop(0, list_count)
     def _(which):
         rows_copy(which).wait()
         here = pl.ds(pl.multiple_of(which * per_list, per_list), per_list)
         scores = mm(rows[which], grouped[here], ROW)
         scores = jnp.where(iota(scores.shape, 0) < fill_ref[which], scores, -jnp.inf)
-        best = jnp.max(scores, axis=0, keepdims=True)
-        hi, mid, low = [term.astype(F32) for term in split(best)]
-        part = iota((8, per_list), 0)
-        parts = jnp.where(part == 0, hi, jnp.where(part == 1, mid, jnp.where(part == 2, low, 0.0)))
-        select = mask(iota((per_list, slots), 0) == bucket_ref[...] - which * per_list)
-        row_ref[...] += jnp.sum(mm(parts.astype(BF16), select), axis=0, keepdims=True)
-
-    mine = jnp.where(iota((cap, 1), 0) == iota((1, slots), 1) % cap, row_ref[...], 0.0)
+        bests_ref[pl.ds(which, 1), :] = jnp.max(scores, axis=0, keepdims=True)
+
+    bucket = bucket_ref[...]
+    terms = jnp.concatenate([term.astype(F32) for term in split(bests_ref[...])], axis=0)
+    found = mm(terms.astype(BF16), mask(iota((per_list, 1), 0) == bucket % per_list))
+    found = sum(found[i * list_count : (i + 1) * list_count] for i in range(3))
+    found = jnp.where(iota((list_count, 1), 0) == bucket // per_list, found, 0.0)
+    found = jnp.sum(found, axis=0, keepdims=True)
+    mine = jnp.where(iota((cap, 1), 0) == iota((1, slots), 1) % cap, found, 0.0)
     spot = mask(iota((count, 1), 0) == iota((1, slots), 1) // cap)
     best = sum(mm(term, spot, ROW) for term in split(mine))
     best = jnp.concatenate([best, jnp.zeros((128 - cap, count), F32)], axis=0)
@@ -274,11 +280,11 @@
     exchange(new_ref, got_new, small_sem.at[2], small_sem.at[3], every, near).wait()
     exchange(vec_ref, got_vec, vec_send, vec_recv.at[0], every, near).wait_send()
     vectors = jnp.concatenate([got_new[:, k, :] for k in range(2)], axis=0)
-    new_ids = jnp.concatenate([ids[cap + 2 + k : cap + 3 + k] for k in range(2)], axis=1).astype(I32)
+    new_ids = jnp.concatenate([ids[2 * cap + 2 + k : 2 * cap + 3 + k] for k in range(2)], axis=1).astype(I32)
     append(new_ids, vectors, count, centroids_ref[...], sums_ref[...], codes_ref, scales_ref, out_ref)
     back_own.wait()
     exchange(best_ref, got_best, back_sem.at[0], back_sem.at[1], every, near).wait()
-    pick(probes_ref, rank_ref, got_best[:, 0, :cap], dup_ref, list_count)
+    max_ref[...] = got_best[:, 0, :]
 
 
 def local(queries, probes, assign, list_rows, list_fill, centroids, list_sums):
@@ -291,17 +297,20 @@
     append_slots = group_size * cap2 // list_count
     slots, slots2 = group_size * cap, group_size * cap2
 
-    table, rank = pl.pallas_call(
+    probes = probes.T
+    table, ids, rank = pl.pallas_call(
         functools.partial(
             route_kernel, group_size=group_size, list_count=list_count, caps=(cap, cap2)
         ),
-        out_shape=(shape((group_size, 128), F32), shape((query_count, probe_count), I32)),
+        out_shape=(
+            shape((group_size, 128), I32),
+            shape((group_size, 1, 128), I32),
+            shape((probe_count, query_count), F32),
+        ),
         in_specs=vmem(2),
-        out_specs=tuple(vmem(2)),
+        out_specs=tuple(vmem(3)),
         name="route",
-    )(probes, assign[:, None])
-    table = table.astype(I32)
-    ids = jnp.pad(table[:, cap : 2 * cap + 2 * cap2], ((0, 0), (0, 128 - cap - 2 * cap2)))[:, None, :]
+    )(probes, assign[None, :])
 
     def chosen(which):
         hot = (which[:, :, None] == jnp.arange(query_count, dtype=I32)).astype(BF16)
@@ -318,20 +327,20 @@
         pltpu.VMEM((list_count, row_count, feature_dim), BF16),
         pltpu.VMEM((slots, feature_dim), BF16),
         pltpu.VMEM((1, slots), I32),
-        pltpu.VMEM((1, slots), F32),
+        pltpu.VMEM((list_count, per_list), F32),
     ]
     DMA = pltpu.SemaphoreType.DMA
-    dup_max, codes, scales, sums = pl.pallas_call(
+    made = pl.pallas_call(
         functools.partial(ingest_kernel, per_list=per_list),
         out_shape=(
-            shape((query_count, probe_count), F32),
+            shape((group_size, 128), F32),
             shape((slots2, feature_dim), BF16),
             shape((list_count, append_slots), F32),
             shape((list_count, feature_dim), F32),
         ),
         in_specs=[
             pl.BlockSpec(memory_space=pltpu.SMEM),
-            *vmem(5),
+            *vmem(3),
             pl.BlockSpec(memory_space=pl.ANY),
             *vmem(2),
         ],
@@ -343,10 +352,20 @@
         ),
         name="ingest",
     )(
-        list_fill, probes, rank, ids, chosen(table[:, 2 * cap : 2 * cap + cap2]),
+        list_fill, ids, chosen(table[:, 2 * cap : 2 * cap + cap2]),
         chosen(table[:, :cap]), list_rows, centroids, list_sums,
     )
-    return dup_max, codes.reshape(list_count, append_slots, feature_dim), scales, sums
+    dup_max, codes, scales, sums = pl.pallas_call(
+        functools.partial(finish_kernel, list_count=list_count, cap=cap),
+        out_shape=(
+            shape((probe_count, query_count), F32),
+            *[shape(one.shape, one.dtype) for one in made[1:]],
+        ),
+        in_specs=vmem(6),
+        out_specs=tuple(vmem(4)),
+        name="finish",
+    )(probes, rank, *made)
+    return dup_max.T, codes.reshape(list_count, append_slots, feature_dim), scales, sums
 
 
 def solution(mesh):

time: 99.4 us -> 85.3 us (0.86)
  local copies, waits for them, and re-layouts: 10.5 us -> 2.89 us
  Pallas kernels: 84.2 us -> 78.7 us
    pallas_call x1, Pallas kernels: 81.1 us -> 72.8 us  [local(): pl.pallas_call(functools.partial(ingest_kernel, per_list=per_list), out_s...]
    unnamed x7 -> x2, local copies, waits for them, and re-layouts: 7.24 us -> 0.01 us
    pallas_call x0 -> x1, Pallas kernels: none -> 2.58 us  [local(): pl.pallas_call(functools.partial(finish_kernel, list_count=list_count, ca...]
    broadcast_in_dim x1 -> x0, local copies, waits for them, and re-layouts: 1.35 us -> none  [local(): assign[:, None]]
where the time goes in v2:
time: 85.3 us; the launch traced here: 85 us
  Pallas kernels  78.7 us (92%)
  local copies, waits for them, and re-layouts  2.89 us (3%)
  matrix products  2.72 us (3%)
    pallas_call x1, Pallas kernels, local(): pl.pallas_call(functools.partial(ingest_kernel, per_list=per_list), out_s...  72.8 us
    pallas_call x1, Pallas kernels, local(): pl.pallas_call(functools.partial(route_kernel, group_size=group_size, lis...  3.39 us
    dot_general x2, matrix products, chosen(): picked = jnp.dot(hot, queries, preferred_element_type=F32).astype(BF16)  2.72 us
    pallas_call x1, Pallas kernels, local(): pl.pallas_call(functools.partial(finish_kernel, list_count=list_count, ca...  2.58 us

profile of v2, /device:TPU:1, one launch (start us, length us, event | category | flops | bytes accessed | tf_op | source)
XLA Modules:
  0.0 85.0 jit_solution(4615919913206727203)
XLA Ops:
  0.6 0.0 copy-start
  0.6 3.4 %route.1 = (s32[128,128]{1,0:T(8,128)}, s32[128,1,128]{2,1,0:T(1,128)}, f32[16,64]{1,0:T(8,128)}) custom-call(s32[16,64]{1,0:T(8,128)} %bitcast.10, s32[1,64]{1,0:T(1,128)} %bitcast.12), custom_call_target="tpu_custom_call" | custom-call | tf_op jit(solution)/shard_map/route/pallas_call | solution.py:301
  4.0 0.9 %eq.36 = s32[2048]{0:T(1024)S(1)} reshape(s32[128,16]{1,0:T(8,128)} %bitcast.9) | data formatting | bytes 16384 | tf_op jit(solution)/shard_map/eq | solution.py:316
  5.0 0.9 %slice.6 = s32[128,2]{1,0:T(8,128)S(1)} slice(s32[128,128]{1,0:T(8,128)} %get-tuple-element.17), slice={[0:128], [32:34]} | slice | bytes 2048 | tf_op jit(solution)/shard_map/slice | solution.py:355
  5.9 0.1 eq.32
  6.0 0.0 copy-done
  6.0 0.3 convolution_convert_fusion.1
  6.3 0.9 %reshape.25.new_ref = bf16[128,2,768]{2,1,0:T(2,128)(2,1)} reshape(bf16[256,768]{1,0:T(8,128)(2,1)S(1)} %convolution_convert_fusion.1) | data formatting | bytes 786432 | tf_op jit(solution)/shard_map/reshape | solution.py:319
  7.2 2.4 %convolution_convert_fusion = bf16[2048,768]{1,0:T(8,128)(2,1)} fusion(bf16[64,768]{1,0:T(8,128)(2,1)S(1)} %copy-done, s32[2048]{0:T(1024)S(1)} %eq.36), kind=kOutput, calls=%fused_computation | convolution fusion | flops 203030528 | bytes 3252224 | tf_op jit(solution)/shard_map/dot_general | solution.py:318
  9.7 72.8 %ingest.1 = (f32[128,128]{1,0:T(8,128)}, bf16[256,768]{1,0:T(8,128)(2,1)}, f32[8,32]{1,0:T(8,128)}, f32[8,768]{1,0:T(8,128)}) custom-call(s32[8]{0:T(128)} %fill_ref.1, s32[128,1,128]{2,1,0:T(1,128)} %get-tuple-element.16.ids_ref, bf16[128,2,768]{2,1,0:T(2,128)(2,1)} %reshape.25.new_ref, bf16[128,16,768]{2,1,0:T(8,128)(2,1)} %bitcast.8, ...), custom_call_target="tpu_custom_call" | custom-call | tf_op jit(solution)/shard_map/ingest/pallas_call | solution.py:333
  82.4 2.6 %finish.1 = (f32[16,64]{1,0:T(8,128)}, bf16[256,768]{1,0:T(8,128)(2,1)}, f32[8,32]{1,0:T(8,128)}, f32[8,768]{1,0:T(8,128)}) custom-call(s32[16,64]{1,0:T(8,128)} %bitcast.11, f32[16,64]{1,0:T(8,128)} %get-tuple-element.15.rank_ref, f32[128,128]{1,0:T(8,128)} %get-tuple-element.18.best_ref, bf16[256,768]{1,0:T(8,128)(2,1)} %get-tuple-element.19.codes_ref, ...), custom_call_target="tpu_custom_call" | custom-call | tf_op jit(solution)/shard_map/finish/pallas_call | solution.py:358
Async XLA Ops:
  0.6 5.4 %copy-start = (bf16[64,768]{1,0:T(8,128)(2,1)S(1)}, bf16[64,768]{1,0:T(8,128)(2,1)}, u32[]{:S(2)}) copy-start(bf16[64,768]{1,0:T(8,128)(2,1)} %param.7) | copy-start | bytes 294916

commit v3 on v2

--- a/solution.py
+++ b/solution.py
@@ -251,9 +251,11 @@
             vectors = got_vec[group * each : (group + 1) * each].reshape(each * cap, feature_dim)
             grouped[here] += mm(select, vectors).astype(BF16)
 
-    @pl.loop(0, list_count)
+    for which in range(list_count):
+        rows_copy(which).wait()
+
+    @pl.loop(0, list_count, unroll=4)
     def _(which):
-        rows_copy(which).wait()
         here = pl.ds(pl.multiple_of(which * per_list, per_list), per_list)
         scores = mm(rows[which], grouped[here], ROW)
         scores = jnp.where(iota(scores.shape, 0) < fill_ref[which], scores, -jnp.inf)

time: 85.3 us -> 84 us (0.985)
  Pallas kernels: 78.7 us -> 77.4 us
    pallas_call x1, Pallas kernels: 72.8 us -> 71.5 us  [local(): pl.pallas_call(functools.partial(ingest_kernel, per_list=per_list), out_s...]
where the time goes in v3:
time: 84 us; the launch traced here: 83.7 us
  Pallas kernels  77.4 us (92%)
  local copies, waits for them, and re-layouts  2.89 us (3%)
  matrix products  2.72 us (3%)
    pallas_call x1, Pallas kernels, local(): pl.pallas_call(functools.partial(ingest_kernel, per_list=per_list), out_s...  71.5 us
    pallas_call x1, Pallas kernels, local(): pl.pallas_call(functools.partial(route_kernel, group_size=group_size, lis...  3.39 us
    dot_general x2, matrix products, chosen(): picked = jnp.dot(hot, queries, preferred_element_type=F32).astype(BF16)  2.72 us
    pallas_call x1, Pallas kernels, local(): pl.pallas_call(functools.partial(finish_kernel, list_count=list_count, ca...  2.58 us

profile of v3, /device:TPU:1, one launch (start us, length us, event | category | flops | bytes accessed | tf_op | source)
XLA Modules:
  0.0 83.7 jit_solution(4132206170002015540)
XLA Ops:
  0.6 0.0 copy-start
  0.6 3.4 %route.1 = (s32[128,128]{1,0:T(8,128)}, s32[128,1,128]{2,1,0:T(1,128)}, f32[16,64]{1,0:T(8,128)}) custom-call(s32[16,64]{1,0:T(8,128)} %bitcast.10, s32[1,64]{1,0:T(1,128)} %bitcast.12), custom_call_target="tpu_custom_call" | custom-call | tf_op jit(solution)/shard_map/route/pallas_call | solution.py:303
  4.0 0.9 %eq.36 = s32[2048]{0:T(1024)S(1)} reshape(s32[128,16]{1,0:T(8,128)} %bitcast.9) | data formatting | bytes 16384 | tf_op jit(solution)/shard_map/eq | solution.py:318
  5.0 0.9 %slice.6 = s32[128,2]{1,0:T(8,128)S(1)} slice(s32[128,128]{1,0:T(8,128)} %get-tuple-element.17), slice={[0:128], [32:34]} | slice | bytes 2048 | tf_op jit(solution)/shard_map/slice | solution.py:357
  5.9 0.1 eq.32
  6.0 0.0 copy-done
  6.0 0.3 convolution_convert_fusion.1
  6.3 0.9 %reshape.25.new_ref = bf16[128,2,768]{2,1,0:T(2,128)(2,1)} reshape(bf16[256,768]{1,0:T(8,128)(2,1)S(1)} %convolution_convert_fusion.1) | data formatting | bytes 786432 | tf_op jit(solution)/shard_map/reshape | solution.py:321
  7.2 2.4 %convolution_convert_fusion = bf16[2048,768]{1,0:T(8,128)(2,1)} fusion(bf16[64,768]{1,0:T(8,128)(2,1)S(1)} %copy-done, s32[2048]{0:T(1024)S(1)} %eq.36), kind=kOutput, calls=%fused_computation | convolution fusion | flops 203030528 | bytes 3252224 | tf_op jit(solution)/shard_map/dot_general | solution.py:320
  9.7 71.5 %ingest.1 = (f32[128,128]{1,0:T(8,128)}, bf16[256,768]{1,0:T(8,128)(2,1)}, f32[8,32]{1,0:T(8,128)}, f32[8,768]{1,0:T(8,128)}) custom-call(s32[8]{0:T(128)} %fill_ref.1, s32[128,1,128]{2,1,0:T(1,128)} %get-tuple-element.16.ids_ref, bf16[128,2,768]{2,1,0:T(2,128)(2,1)} %reshape.25.new_ref, bf16[128,16,768]{2,1,0:T(8,128)(2,1)} %bitcast.8, ...), custom_call_target="tpu_custom_call" | custom-call | tf_op jit(solution)/shard_map/ingest/pallas_call | solution.py:335
  81.2 2.6 %finish.1 = (f32[16,64]{1,0:T(8,128)}, bf16[256,768]{1,0:T(8,128)(2,1)}, f32[8,32]{1,0:T(8,128)}, f32[8,768]{1,0:T(8,128)}) custom-call(s32[16,64]{1,0:T(8,128)} %bitcast.11, f32[16,64]{1,0:T(8,128)} %get-tuple-element.15.rank_ref, f32[128,128]{1,0:T(8,128)} %get-tuple-element.18.best_ref, bf16[256,768]{1,0:T(8,128)(2,1)} %get-tuple-element.19.codes_ref, ...), custom_call_target="tpu_custom_call" | custom-call | tf_op jit(solution)/shard_map/finish/pallas_call | solution.py:360
Async XLA Ops:
  0.6 5.4 %copy-start = (bf16[64,768]{1,0:T(8,128)(2,1)S(1)}, bf16[64,768]{1,0:T(8,128)(2,1)}, u32[]{:S(2)}) copy-start(bf16[64,768]{1,0:T(8,128)(2,1)} %param.7) | copy-start | bytes 294916
